TPU v7x, 512 devices: a whole 4x4x16 slice. The times are simulated.
512 devices in a mesh: row: 16 (over y_lo, x, core), col: 32 (over z, y_hi).
Axes of the slice: x: 4, y: 4 (y_hi: 2, y_lo: 2; y = y_hi * 2 + y_lo), z: 16, core: 2. Of those that a mesh axis runs over, the one named last changes fastest.
Arguments:
- coefficients: float32 [8, 8192, 8192], P(None, 'row', 'col'), may hold values from -40 to 40, as said below
- lambdas: float32 [256], replicated, may hold values from -0.95 to 0.95
- right_vecs: float32 [8192, 256], P(('col', 'row')), may hold values from -6 to 6
- left_vecs: float32 [8192, 256], P(('row', 'col')), may hold values from -6 to 6
Outputs:
- right_resid: float32 [8192, 256], P(('row', 'col'))
- left_resid: float32 [8192, 256], P(('col', 'row'))
- root_mean: float32 [2, 256], replicated
Inputs may be any that keep to these rules, and one draw needn't show every extreme that they name: `coefficients`: the entries of every coefficient matrix.
All inputs are finite; a program needn't handle non-finite values.
Results may differ from a plain program's by a relative error of at most 0.0001.
Values sent between devices are 32-bit elements; how exact they have to be, the bound alone decides.
A program may use at most 64 MiB of HBM per device.

v0:
```python
import jax
import jax.numpy as jnp
from jax import lax
from jax.sharding import PartitionSpec as P

N = 8192
epsilon = 1e-06


def chebyshev(lambdas, count):
    terms = [jnp.ones_like(lambdas), lambdas]
    while len(terms) < count:
        terms.append(2.0 * lambdas * terms[-1] - terms[-2])
    return jnp.stack(terms[:count])


def right_term(matrices, weighted):
    total = jnp.dot(
        matrices[0],
        weighted[0],
        precision=lax.Precision.HIGHEST,
        preferred_element_type=jnp.float32,
    )
    for term in range(1, matrices.shape[0]):
        total = total + jnp.dot(
            matrices[term],
            weighted[term],
            precision=lax.Precision.HIGHEST,
            preferred_element_type=jnp.float32,
        )
    return total


def left_term(matrices, weighted):
    numbers = (((0,), (0,)), ((), ()))
    total = lax.dot_general(
        matrices[0],
        weighted[0],
        numbers,
        precision=lax.Precision.HIGHEST,
        preferred_element_type=jnp.float32,
    )
    for term in range(1, matrices.shape[0]):
        total = total + lax.dot_general(
            matrices[term],
            weighted[term],
            numbers,
            precision=lax.Precision.HIGHEST,
            preferred_element_type=jnp.float32,
        )
    return total


def body(coefficients, lambdas, right_vecs, left_vecs):
    weights = chebyshev(lambdas, coefficients.shape[0])
    right_cols = lax.all_gather(right_vecs, "row", axis=0, tiled=True)
    left_rows = lax.all_gather(left_vecs, "col", axis=0, tiled=True)
    right_weighted = right_cols[None, :, :] * weights[:, None, :]
    left_weighted = left_rows[None, :, :] * weights[:, None, :]
    matrices = coefficients
    right_resid = lax.psum_scatter(
        right_term(matrices, right_weighted), "col", scatter_dimension=0, tiled=True
    )
    matrices = coefficients
    left_resid = lax.psum_scatter(
        left_term(matrices, left_weighted), "row", scatter_dimension=0, tiled=True
    )
    right_squares, left_squares = lax.psum(
        (jnp.sum(right_resid * right_resid, axis=0), jnp.sum(left_resid * left_resid, axis=0)),
        ("row", "col"),
    )
    root_mean = jnp.sqrt(jnp.stack([right_squares, left_squares]) / N + epsilon)
    return (right_resid, left_resid, root_mean)


def solution(mesh):
    return jax.shard_map(
        body,
        mesh=mesh,
        in_specs=(P(None, "row", "col"), P(), P(("col", "row"), None), P(("row", "col"), None)),
        out_specs=(P(("row", "col"), None), P(("col", "row"), None), P()),
        check_vma=False,
    )
```

profile of v0, /device:TPU:1, one launch (start us, length us, event | category | flops | bytes accessed | tf_op | source)
XLA Modules:
  0.0 924.4 jit_solution(9988181470796313399)
XLA Ops:
  7.2 0.0 reduce-scatter.9.cloned.1.call-start
  7.2 0.7 multiply_subtract_fusion
  7.9 0.7 multiply_subtract_fusion.1
  8.6 72.7 %all_gather.7 = f32[512,256]{1,0:T(8,128)S(1)} all-gather(f32[16,256]{1,0:T(8,128)} %param.7), channel_id=1, replica_groups=mesh['row'=16,'col'=32] {'col'}, dimensions={0}, use_global_device_ids=true | all-gather | bytes 540672 | tf_op jit(solution)/shard_map/all_gather | solution.py:57
  81.3 0.7 stack.40
  82.0 0.0 copy-start
  82.0 0.4 broadcast_multiply_fusion
  82.4 1.8 copy-done
  84.2 1.0 fusion.2
  85.3 1.0 convolution_add_fusion.13
  86.3 1.0 convolution_add_fusion.12
  87.3 0.0 copy-start.2
  87.3 1.0 convolution_add_fusion.11
  88.4 1.0 convolution_add_fusion.10
  89.4 1.0 convolution_add_fusion.9
  90.4 1.0 convolution_add_fusion.8
  91.5 1.0 fusion.1
  92.5 0.8 copy.13
  93.4 0.0 reduce-scatter.9.cloned.1.call-update
  93.4 0.0 reduce-scatter.7.cloned.1.call-start
  93.4 0.0 copy-done.2
  93.4 0.0 copy-start.1
  93.5 34.1 %all_gather.6 = f32[256,256]{1,0:T(8,128)S(1)} all-gather(f32[16,256]{1,0:T(8,128)S(1)} %copy-done.2), channel_id=1, replica_groups=mesh['row'=16,'col'=32] {'row'}, dimensions={0}, use_global_device_ids=true | all-gather | bytes 278528 | tf_op jit(solution)/shard_map/all_gather | solution.py:56
  127.5 0.2 broadcast_multiply_fusion.1
  127.7 2.1 fusion.18
  129.8 2.1 convolution_add_fusion.6
  131.9 0.0 copy-done.1
  131.9 1.0 convolution_add_fusion.5
  133.0 1.0 convolution_add_fusion.4
  134.0 1.0 convolution_add_fusion.3
  135.1 1.0 convolution_add_fusion.2
  136.1 1.0 convolution_add_fusion.1
  137.2 1.0 fusion
  138.2 1.0 copy.11
  139.2 0.0 reduce-scatter.7.cloned.1.call-update
  139.2 27.8 %reduce-scatter.9.cloned.1.call-done = f32[16,256]{1,0:T(8,128)} async-done(((f32[256,256]{1,0:T(8,128)}), f32[16,256]{1,0:T(8,128)}) %reduce-scatter.9.cloned.1.call-update) | async-done | bytes 16400
  167.0 0.8 copy.14
  167.9 0.1 multiply_reduce_fusion
  168.0 635.2 %reduce-scatter.7.cloned.1.call-done = f32[16,256]{1,0:T(8,128)} async-done(((f32[512,256]{1,0:T(8,128)}), f32[16,256]{1,0:T(8,128)}) %reduce-scatter.7.cloned.1.call-update) | async-done | bytes 16400
  803.2 0.8 copy.12
  804.0 0.1 multiply_reduce_fusion.1
  804.1 112.8 %all-reduce = (f32[1,256]{1,0:T(1,128)S(1)}, f32[1,256]{1,0:T(1,128)S(1)}) all-reduce(f32[1,256]{1,0:T(1,128)S(1)} %bitcast.105, f32[1,256]{1,0:T(1,128)S(1)} %bitcast.106), channel_id=1, replica_groups=mesh['row'=16,'col'=32] {'row','col'}, use_global_device_ids=true, to_apply=%region_5.0 | all-reduce | flops 512 | bytes 4096 | tf_op jit(solution)/shard_map/psum | solution.py:68
  916.9 0.6 fusion.37
  (1 shorter events, 0.0 us)
Async XLA Ops:
  7.2 159.9 %reduce-scatter.9.cloned.1.call-start = ((), (), s32[]{:S(2)}) async-start(), calls=%async_computation.3 | async-start | bytes 278528
  82.0 2.2 copy-start
  87.3 6.1 copy-start.2
  93.4 709.8 %reduce-scatter.7.cloned.1.call-start = ((), (), s32[]{:S(2)}) async-start(), calls=%async_computation.2 | async-start | bytes 540672
  93.4 38.5 %copy-start.1 = (f32[8,512,256]{2,1,0:T(8,128)S(1)}, f32[8,512,256]{2,1,0:T(8,128)}, u32[]{:S(2)}) copy-start(f32[8,512,256]{2,1,0:T(8,128)} %param.4) | copy-start | bytes 12582916
Sparse Core Ops, SparseCore 0:
  93.5 73.4 reduce-scatter.8
  172.0 631.1 reduce-scatter.6
where the time goes:
time: 925 us; the launch traced here: 924 us
  waiting for transfers between devices  663 us (72%)
  blocking collectives  220 us (24%)
  matrix products  18.7 us (2%)
  between operations  14.2 us (2%)
    unnamed x4, waiting for transfers between devices  663 us
    psum x1, blocking collectives, body(): lax.psum((jnp.sum(right_resid * right_resid, axis=0), jnp.sum(left_resid...  113 us
    all_gather x1, blocking collectives, body(): left_rows = lax.all_gather(left_vecs, 'col', axis=0, tiled=True)  72.7 us
    all_gather x1, blocking collectives, body(): right_cols = lax.all_gather(right_vecs, 'row', axis=0, tiled=True)  34.1 us
  transfers between devices with their start and end apart: 2, of which 2 were waited for; matrix products, arithmetic and copies ran while one was open for 1% of the time, Pallas kernels for 0%

commit v1 on v0

--- a/solution.py
+++ b/solution.py
@@ -1,3 +1,4 @@
+import functools
 import jax
 import jax.numpy as jnp
 from jax import lax
@@ -5,6 +6,22 @@
 
 N = 8192
 epsilon = 1e-06
+
+
+def solve_the_targets(local_array, axis_key):
+    k_now = jnp.concatenate(
+        lax.all_to_all(
+            jnp.stack(lax.axis_size(axis_key) * [local_array]),
+            axis_name=axis_key,
+            split_axis=0,
+            concat_axis=0,
+        ),
+        axis=0,
+    )
+    return k_now
+
+
+get_spot = functools.partial(solve_the_targets, axis_key="col")
 
 
 def chebyshev(lambdas, count):
@@ -54,7 +71,7 @@
 def body(coefficients, lambdas, right_vecs, left_vecs):
     weights = chebyshev(lambdas, coefficients.shape[0])
     right_cols = lax.all_gather(right_vecs, "row", axis=0, tiled=True)
-    left_rows = lax.all_gather(left_vecs, "col", axis=0, tiled=True)
+    left_rows = get_spot(left_vecs)
     right_weighted = right_cols[None, :, :] * weights[:, None, :]
     left_weighted = left_rows[None, :, :] * weights[:, None, :]
     matrices = coefficients

time: 925 us -> 884 us (0.956)
  blocking collectives: 220 us -> 127 us
  waiting for transfers between devices: 663 us -> 694 us
  starting transfers between devices: 0.08 us -> 18.9 us
    all_gather x1 -> x0, blocking collectives: 72.7 us -> none  [body(): left_rows = lax.all_gather(left_vecs, 'col', axis=0, tiled=True)]
    unnamed x4, waiting for transfers between devices: 663 us -> 694 us
    all_to_all x0 -> x1, starting transfers between devices: none -> 18.6 us  [solve_the_targets(): lax.all_to_all(jnp.stack(lax.axis_size(axis_key) * [local_array]), axis_n...]
    all_gather x1, blocking collectives: 34.1 us -> 20.6 us  [body(): right_cols = lax.all_gather(right_vecs, 'row', axis=0, tiled=True)]
  transfers between devices with their start and end apart: 2 -> 3, of which waited for: 2 -> 2; matrix products, arithmetic and copies ran while one was open for 1% -> 3% of each run, Pallas kernels for 0% -> 0%
where the time goes in v1:
time: 884 us; the launch traced here: 883 us
  waiting for transfers between devices  694 us (79%)
  blocking collectives  127 us (14%)
  starting transfers between devices  18.9 us (2%)
  matrix products  18.8 us (2%)
  between operations  14.2 us (2%)
    unnamed x4, waiting for transfers between devices  694 us
    psum x1, blocking collectives, body(): lax.psum((jnp.sum(right_resid * right_resid, axis=0), jnp.sum(left_resid...  106 us
    all_gather x1, blocking collectives, body(): right_cols = lax.all_gather(right_vecs, 'row', axis=0, tiled=True)  20.6 us
    all_to_all x1, starting transfers between devices, solve_the_targets(): lax.all_to_all(jnp.stack(lax.axis_size(axis_key) * [local_array]), axis_n...  18.6 us
  transfers between devices with their start and end apart: 3, of which 2 were waited for; matrix products, arithmetic and copies ran while one was open for 3% of the time, Pallas kernels for 0%

profile of v1, /device:TPU:1, one launch (start us, length us, event | category | flops | bytes accessed | tf_op | source)
XLA Modules:
  0.0 883.3 jit_solution(4086444135071189958)
XLA Ops:
  7.2 1.6 stack.32
  8.8 18.6 %all-to-all-start = ((f32[32,16,256]{2,1,0:T(8,128)}), f32[32,16,256]{2,1,0:T(8,128)S(1)}, u32[]{:S(2)}, u32[]{:S(2)}) async-start(f32[32,16,256]{2,1,0:T(8,128)} %stack.32), calls=%async_computation | async-start | bytes 1048576 | tf_op jit(solution)/shard_map/all_to_all | solution.py:13
  27.4 0.0 reduce-scatter.7.cloned.1.call-start
  27.5 0.7 multiply_subtract_fusion
  28.2 0.7 multiply_subtract_fusion.1
  28.8 20.6 %all_gather.3 = f32[256,256]{1,0:T(8,128)S(1)} all-gather(f32[16,256]{1,0:T(8,128)} %param.6), channel_id=1, replica_groups=mesh['row'=16,'col'=32] {'row'}, dimensions={0}, use_global_device_ids=true | all-gather | bytes 278528 | tf_op jit(solution)/shard_map/all_gather | solution.py:73
  49.5 0.7 stack.31
  50.2 0.0 copy-start
  50.2 0.2 broadcast_multiply_fusion.1
  50.3 2.2 fusion.18
  52.6 2.1 convolution_add_fusion.6
  54.7 0.0 copy-done
  54.7 1.0 convolution_add_fusion.5
  55.7 1.0 convolution_add_fusion.4
  56.8 1.0 convolution_add_fusion.3
  57.9 1.0 convolution_add_fusion.2
  58.9 1.0 convolution_add_fusion.1
  60.0 1.0 fusion
  61.0 1.0 copy.11
  62.0 0.0 reduce-scatter.7.cloned.1.call-update
  62.0 0.2 reduce-scatter.9.cloned.1.call-start
  62.3 0.0 all-to-all-done
  62.3 0.0 copy-start.1
  62.3 0.4 broadcast_multiply_fusion
  62.6 1.8 copy-done.1
  64.5 1.0 fusion.2
  65.5 1.0 convolution_add_fusion.13
  66.5 1.0 convolution_add_fusion.12
  67.6 1.0 convolution_add_fusion.11
  68.6 1.0 convolution_add_fusion.10
  69.6 1.0 convolution_add_fusion.9
  70.7 1.0 convolution_add_fusion.8
  71.7 1.0 fusion.1
  72.7 0.8 copy.13
  73.6 0.0 reduce-scatter.9.cloned.1.call-update
  73.6 617.2 %reduce-scatter.7.cloned.1.call-done = f32[16,256]{1,0:T(8,128)} async-done(((f32[512,256]{1,0:T(8,128)}), f32[16,256]{1,0:T(8,128)}) %reduce-scatter.7.cloned.1.call-update) | async-done | bytes 16400
  690.8 0.8 copy.12
  691.6 0.1 multiply_reduce_fusion.1
  691.7 77.1 %reduce-scatter.9.cloned.1.call-done = f32[16,256]{1,0:T(8,128)} async-done(((f32[256,256]{1,0:T(8,128)}), f32[16,256]{1,0:T(8,128)}) %reduce-scatter.9.cloned.1.call-update) | async-done | bytes 16400
  768.8 0.8 copy.14
  769.7 0.1 multiply_reduce_fusion
  769.8 106.1 %all-reduce = (f32[1,256]{1,0:T(1,128)S(1)}, f32[1,256]{1,0:T(1,128)S(1)}) all-reduce(f32[1,256]{1,0:T(1,128)S(1)} %bitcast.108, f32[1,256]{1,0:T(1,128)S(1)} %bitcast.107), channel_id=1, replica_groups=mesh['row'=16,'col'=32] {'row','col'}, use_global_device_ids=true, to_apply=%region_5.0 | all-reduce | flops 512 | bytes 4096 | tf_op jit(solution)/shard_map/psum | solution.py:85
  875.9 0.6 fusion.37
  (1 shorter events, 0.0 us)
Async XLA Ops:
  8.8 53.5 %all-to-all-start = ((f32[32,16,256]{2,1,0:T(8,128)}), f32[32,16,256]{2,1,0:T(8,128)S(1)}, u32[]{:S(2)}, u32[]{:S(2)}) async-start(f32[32,16,256]{2,1,0:T(8,128)} %stack.32), calls=%async_computation | async-start | bytes 1048576 | tf_op jit(solution)/shard_map/all_to_all | solution.py:13
  27.4 663.4 %reduce-scatter.7.cloned.1.call-start = ((), (), s32[]{:S(2)}) async-start(), calls=%async_computation.3 | async-start | bytes 540672
  50.2 4.5 copy-start
  62.0 706.8 %reduce-scatter.9.cloned.1.call-start = ((), (), s32[]{:S(2)}) async-start(), calls=%async_computation.4 | async-start | bytes 278528
  62.3 2.2 copy-start.1
Sparse Core Ops, SparseCore 0:
  62.1 628.5 reduce-scatter.6
  694.1 74.6 reduce-scatter.8
